TPU v7x, 32 devices: a whole 2x2x4 slice. The times are simulated.
32 devices in a mesh: dp: 2 (over x), expert: 16 (over z, y, core).
Axes of the slice: x: 2, y: 2, z: 4, core: 2. Of those that a mesh axis runs over, the one named last changes fastest.
Arguments:
- q_latent: bfloat16 [128, 16, 576], P(('expert', 'dp')), may hold values from -48 to 48
- latent_cache: bfloat16 [128, 512, 576], P(('expert', 'dp')), may hold values from -10 to 10
- lengths: int32 [128], P(('expert', 'dp')), may hold values from 2 to 512
- residual: bfloat16 [128, 2048], P(('expert', 'dp')), may hold values from -6 to 6
- adapter_ids: int32 [128], P(('expert', 'dp')), may hold values from 0 to 31
- value_out: bfloat16 [8192, 2048], P('expert'), may hold values from -0.0625 to 0.0625
- adapter_down: bfloat16 [8192, 512], P('expert'), may hold values from -0.0625 to 0.0625
- adapter_up_factors: bfloat16 [512, 2048], P('expert'), may hold values from -1.5 to 1.5
- norm_gain: bfloat16 [2048], replicated, may hold values from 0.099609375 to 1.8984375
- expert_ids: int32 [128, 6], P('expert'), may hold values from 0 to 15, all different within a row; in each aligned block of 8 rows (0 to 7, 8 to 15, ...) at most 6 rows name the same one
- gate_weights: float32 [128, 6], P('expert'), may hold values from 0.05 to 0.5
- w_gate: bfloat16 [16, 2048, 1024], P('expert', None, 'dp'), may hold values from -0.125 to 0.125
- w_up: bfloat16 [16, 2048, 1024], P('expert', None, 'dp'), may hold values from -0.125 to 0.125
- w_down: bfloat16 [16, 2048, 1024], P('expert', None, 'dp'), may hold values from -0.1875 to 0.1875
Outputs:
- layer_out: bfloat16 [128, 2048], P(('expert', 'dp'))
Inputs may be any that keep to these rules, and one draw needn't show every extreme that they name: `expert_ids`: each row names 6 different experts. Requests e * 8 to e * 8 + 7 form aligned blocks; in each block no expert is named by more than 6 rows, and in some block an expert is named by exactly 6 rows.
All inputs are finite; a program needn't handle non-finite values.
Results may differ from a plain program's by a relative error of at most 0.008.
Values may be sent and summed in bfloat16 or wider, within the bound.
A program may use at most 64 MiB of HBM per device.

v0:
```python
import jax
import jax.numpy as jnp
from jax import lax
from jax.sharding import PartitionSpec as P

LAT = 512
ADAPTER_RANK = 16


SOFTMAX_SCALE = 192.0 ** (-0.5)
ADAPTER_SCALE = 2.0
EPSILON = 1e-06


def attend_one(query, latent_rows, length):
    scores = (
        lax.dot_general(
            query, latent_rows, (((1,), (1,)), ((), ())), preferred_element_type=jnp.float32
        )
        * SOFTMAX_SCALE
    )
    valid_mask = jnp.arange(latent_rows.shape[0], dtype=jnp.int32) < length
    scores = jnp.where(valid_mask[None, :], scores, -1e30)
    row_max = jnp.max(scores, axis=1, keepdims=True)
    raised = jnp.exp(scores - row_max)
    weights_bf = (raised / jnp.sum(raised, axis=1, keepdims=True)).astype(jnp.bfloat16)
    return jnp.dot(weights_bf, latent_rows[:, :LAT], preferred_element_type=jnp.float32).astype(
        jnp.bfloat16
    )


def expert_rows(tokens, gate_part, up_part, down_part):
    gate_act = jnp.dot(tokens, gate_part, preferred_element_type=jnp.float32)
    up_act = jnp.dot(tokens, up_part, preferred_element_type=jnp.float32)
    hidden_bf = (jax.nn.silu(gate_act) * up_act).astype(jnp.bfloat16)
    return lax.dot_general(
        hidden_bf, down_part, (((1,), (1,)), ((), ())), preferred_element_type=jnp.float32
    )


def local(
    q_latent,
    latent_cache,
    lengths,
    residual,
    adapter_ids,
    value_out,
    adapter_down,
    adapter_up_factors,
    norm_gain,
    expert_ids,
    gate_weights,
    w_gate,
    w_up,
    w_down,
):
    requests = residual.shape[0]
    model_width = residual.shape[1]
    head_count = q_latent.shape[1]
    latent_out = jax.vmap(attend_one)(q_latent, latent_cache, lengths).reshape(
        requests, head_count * LAT
    )
    pieces = lax.all_to_all(latent_out, "expert", split_axis=1, concat_axis=0, tiled=True)
    group_ids = lax.all_gather(adapter_ids, "expert", axis=0, tiled=True)
    group_rows = pieces.shape[0]
    adapters = adapter_down.shape[1] // ADAPTER_RANK
    owned_count = adapter_up_factors.shape[0] // ADAPTER_RANK
    down_projected_rows = jnp.dot(pieces, adapter_down, preferred_element_type=jnp.float32).reshape(
        group_rows, adapters, ADAPTER_RANK
    )
    chosen_adapters = group_ids[:, None] == jnp.arange(adapters, dtype=jnp.int32)[None, :]
    adapter_output = jnp.sum(
        jnp.where(chosen_adapters[:, :, None], down_projected_rows, 0.0), axis=1
    )
    adapter_down_rows = lax.psum(adapter_output, "expert")
    adapter_scaled_output = (ADAPTER_SCALE * adapter_down_rows).astype(jnp.bfloat16)
    first_owned = lax.axis_index("expert") * owned_count
    holder_mask = (
        group_ids[:, None] == first_owned + jnp.arange(owned_count, dtype=jnp.int32)[None, :]
    )
    spread_rows = jnp.where(
        holder_mask[:, :, None], adapter_scaled_output[:, None, :], jnp.zeros((), jnp.bfloat16)
    ).reshape(group_rows, owned_count * ADAPTER_RANK)
    attention = lax.psum_scatter(
        jnp.dot(pieces, value_out, preferred_element_type=jnp.float32)
        + jnp.dot(spread_rows, adapter_up_factors, preferred_element_type=jnp.float32),
        "expert",
        scatter_dimension=0,
        tiled=True,
    )
    residual_flow = residual.astype(jnp.float32) + attention
    inverse_rms = lax.rsqrt(
        jnp.mean(residual_flow * residual_flow, axis=1, keepdims=True) + EPSILON
    )
    normed = (residual_flow * inverse_rms * norm_gain.astype(jnp.float32)).astype(jnp.bfloat16)
    column = lax.all_gather(normed, "dp", axis=0, tiled=True)
    tokens = column.shape[0]
    top_count = expert_ids.shape[1]
    experts = lax.axis_size("expert") * w_gate.shape[0]
    share_size = max(1, 2 * requests * top_count // experts)
    dp_count = lax.axis_size("dp")
    slot_count = share_size * dp_count
    member = expert_ids[:, :, None] == jnp.arange(experts, dtype=jnp.int32)[None, None, :]
    flat_hits = member.reshape(tokens * top_count, experts).astype(jnp.int32)
    slot_rank = jnp.sum((jnp.cumsum(flat_hits, axis=0) - 1) * flat_hits, axis=1).reshape(
        tokens, top_count
    )
    placed = member[:, :, :, None] & (
        slot_rank[:, :, None, None] == jnp.arange(slot_count, dtype=jnp.int32)[None, None, None, :]
    )
    routing = jnp.any(placed, axis=1).reshape(tokens, experts * slot_count)
    combine = jnp.sum(jnp.where(placed, gate_weights[:, :, None, None], 0.0), axis=1).reshape(
        tokens, experts * slot_count
    )
    routing_rows = routing.T.astype(jnp.bfloat16)
    outgoing = (
        jnp.dot(routing_rows, column, preferred_element_type=jnp.float32)
        .astype(jnp.bfloat16)
        .reshape(experts, slot_count, model_width)
    )
    arrived = lax.all_to_all(outgoing, "expert", split_axis=0, concat_axis=0, tiled=True)
    produced = expert_rows(arrived.reshape(-1, model_width), w_gate[0], w_up[0], w_down[0])
    partial_value = produced.reshape(arrived.shape[0], arrived.shape[1], model_width)
    returned = lax.all_to_all(
        partial_value.astype(jnp.bfloat16), "expert", split_axis=0, concat_axis=0, tiled=True
    ).astype(partial_value.dtype)
    routed_column = jnp.dot(
        combine,
        returned.reshape(experts * slot_count, model_width),
        precision=lax.Precision.HIGHEST,
        preferred_element_type=jnp.float32,
    )
    routed_sum = lax.psum_scatter(
        routed_column.astype(jnp.bfloat16), "dp", scatter_dimension=0, tiled=True
    ).astype(jnp.float32)
    return (residual_flow + routed_sum).astype(jnp.bfloat16)


def solution(mesh):
    in_specs = (
        P(("expert", "dp"), None, None),
        P(("expert", "dp"), None, None),
        P(("expert", "dp")),
        P(("expert", "dp"), None),
        P(("expert", "dp")),
        P("expert", None),
        P("expert", None),
        P("expert", None),
        P(),
        P("expert", None),
        P("expert", None),
        P("expert", None, "dp"),
        P("expert", None, "dp"),
        P("expert", None, "dp"),
    )
    out_specs = P(("expert", "dp"), None)
    return jax.shard_map(local, mesh=mesh, in_specs=in_specs, out_specs=out_specs, check_vma=False)
```

profile of v0, /device:TPU:0, one launch (start us, length us, event | category | flops | bytes accessed | tf_op | source)
XLA Modules:
  0.0 223.4 jit_solution(10527450560244738211)
XLA Ops:
  6.5 0.9 iota_compare_fusion.4
  7.4 2.1 fusion.17
  9.6 0.2 fusion.31
  9.8 2.3 %fusion.19 = bf16[4,16,512]{2,1,0:T(8,128)(2,1)S(1)} fusion(bf16[4,512,576]{1,2,0:T(8,128)(2,1)} %param.15, f32[4,16]{1,0:T(4,128)S(1)} %fusion.31, f32[4,16,512]{2,1,0:T(8,128)S(1)} %fusion.17), kind=kOutput, calls=%fused_computation.21 | convolution fusion | flops 33686080 | bytes 2426880 | tf_op jit(solution)/shard_map/vmap()/dot_general | solution.py:27
  12.1 0.7 copy.29
  12.8 7.4 %all-to-all-start = ((bf16[4,16,512]{2,0,1:T(4,128)(2,1)}), bf16[4,16,512]{2,0,1:T(4,128)(2,1)S(1)}, u32[]{:S(2)}, u32[]{:S(2)}) async-start(bf16[4,16,512]{2,0,1:T(4,128)(2,1)} %copy.29), calls=%async_computation | async-start | bytes 131072 | tf_op jit(solution)/shard_map/all_to_all | solution.py:63
  20.2 0.0 all-reduce.5.cloned.1.call-start
  20.3 0.1 eq.89
  20.3 0.1 copy.32
  20.4 0.6 fusion.30
  21.7 0.2 dynamic-update-slice
  21.9 12.4 %all-reduce = s32[64]{0:T(128)S(1)} all-reduce(s32[64]{0:T(128)S(1)} %dynamic-update-slice), channel_id=1, replica_groups=mesh['dp'=2,'expert'=16] {'expert'}, use_global_device_ids=true, to_apply=%add | all-reduce | flops 64 | bytes 512
  34.3 0.2 copy.30
  34.6 0.1 fusion.27
  34.7 0.1 reduce_window_sum.11
  34.7 0.2 select_reduce_fusion
  34.9 0.1 eq.93
  35.0 0.1 copy.33
  35.1 0.1 broadcast_compare_fusion
  35.2 0.5 fusion.16
  35.7 30.0 %psum.7 = f32[64,16]{0,1:T(8,128)S(1)} all-reduce(f32[64,16]{0,1:T(8,128)S(1)} %fusion.16), channel_id=1, replica_groups=mesh['dp'=2,'expert'=16] {'expert'}, use_global_device_ids=true, to_apply=%region_3.4 | all-reduce | flops 1024 | bytes 8192 | tf_op jit(solution)/shard_map/psum | solution.py:75
  65.7 2.1 fusion.32
  67.8 1.1 convolution_add_fusion
  68.9 0.0 all-reduce.5.cloned.1.call-update
  68.9 0.1 iota_compare_fusion.2
  69.0 0.1 and_reduce_fusion
  69.1 0.1 copy.35
  69.3 0.1 reshape.121
  70.0 87.0 %all-reduce.5.cloned.1.call-done = f32[64,2048]{1,0:T(8,128)} async-done(((f32[64,2048]{1,0:T(8,128)}), f32[64,2048]{1,0:T(8,128)}) %all-reduce.5.cloned.1.call-update) | async-done | bytes 524304
  157.0 1.0 multiply_reduce_fusion
  158.0 0.9 fusion.28
  158.9 4.4 %all-gather = bf16[2,4,2048]{2,1,0:T(4,128)(2,1)S(1)} all-gather(bf16[1,4,2048]{2,1,0:T(4,128)(2,1)S(1)} %fusion.28), channel_id=1, replica_groups=mesh['dp'=2,'expert'=16] {'dp'}, dimensions={0}, use_global_device_ids=true | all-gather | bytes 49152 | tf_op jit(solution)/shard_map/all_gather | solution.py:96
  163.3 0.3 convolution_convert_fusion.1
  163.7 0.1 reshape.122
  163.8 19.2 %all_to_all.26 = bf16[16,6,2048]{2,1,0:T(8,128)(2,1)S(1)} all-to-all(bf16[16,6,2048]{2,1,0:T(8,128)(2,1)S(1)} %reshape.122), channel_id=1, replica_groups=mesh['dp'=2,'expert'=16] {'expert'}, dimensions={0} | all-to-all | bytes 786432 | tf_op jit(solution)/shard_map/all_to_all | solution.py:121
  183.0 0.1 reshape.123
  183.2 2.2 fusion.5
  185.4 0.5 fusion.13
  186.0 0.8 convolution_convert_fusion
  186.7 1.0 copy.37
  187.8 4.2 %all-to-all-start.2 = ((bf16[16,6,2048]{2,1,0:T(8,128)(2,1)}), bf16[16,6,2048]{2,1,0:T(8,128)(2,1)S(1)}, u32[]{:S(2)}, u32[]{:S(2)}) async-start(bf16[16,6,2048]{2,1,0:T(8,128)(2,1)} %copy.37), calls=%async_computation.2 | async-start | bytes 1048576 | tf_op jit(solution)/shard_map/all_to_all | solution.py:124
  191.9 0.1 copy.34
  192.0 0.6 dynamic-slice.3
  193.3 0.1 fusion.24
  193.4 12.8 %all-to-all-done.2 = bf16[16,6,2048]{2,1,0:T(8,128)(2,1)S(1)} async-done(((bf16[16,6,2048]{2,1,0:T(8,128)(2,1)}), bf16[16,6,2048]{2,1,0:T(8,128)(2,1)S(1)}, u32[]{:S(2)}, u32[]{:S(2)}) %all-to-all-start.2) | async-done | bytes 393248 | tf_op jit(solution)/shard_map/all_to_all | solution.py:124
  206.2 0.6 fusion.1
  206.8 8.3 %all-reduce.2 = bf16[8,2048]{1,0:T(8,128)(2,1)S(1)} all-reduce(bf16[8,2048]{1,0:T(8,128)(2,1)S(1)} %fusion.1), channel_id=3, replica_groups=mesh['dp'=2,'expert'=16] {'dp'}, use_global_device_ids=true, to_apply=%region_10.11.clone | all-reduce | flops 16384 | bytes 65536
  215.1 1.5 add_convert_fusion
  (35 shorter events, 0.2 us)
Async XLA Ops:
  6.5 179.4 %copy-start = (bf16[1,2048,512]{2,1,0:T(8,128)(2,1)S(1)}, bf16[1,2048,512]{2,1,0:T(8,128)(2,1)}, u32[]{:S(2)}) copy-start(bf16[1,2048,512]{2,1,0:T(8,128)(2,1)} %param.27) | copy-start | bytes 6291460
  9.6 10.7 %copy-start.4 = (s32[8,6]{1,0:T(8,128)S(1)}, s32[8,6]{1,0:T(8,128)}, u32[]{:S(2)}) copy-start(s32[8,6]{1,0:T(8,128)} %param.23) | copy-start | bytes 580
  9.6 10.8 %copy-start.7 = (u32[32]{0:T(128)S(1)}, u32[32]{0:T(128)}, u32[]{:S(2)}) copy-start(u32[32]{0:T(128)} %constant.49) | copy-start | bytes 388
  9.6 12.1 %copy-start.9 = (s32[4]{0:T(128)S(1)}, s32[4]{0:T(128)}, u32[]{:S(2)}) copy-start(s32[4]{0:T(128)} %param.18) | copy-start | bytes 52
  9.6 24.7 %copy-start.1 = (bf16[512,512]{1,0:T(8,128)(2,1)S(1)}, bf16[512,512]{1,0:T(8,128)(2,1)}, u32[]{:S(2)}) copy-start(bf16[512,512]{1,0:T(8,128)(2,1)} %param.20) | copy-start | bytes 1572868
  9.6 25.0 %copy-start.5 = (bf16[2048]{0:T(1024)(128)(2,1)S(1)}, bf16[2048]{0:T(1024)(128)(2,1)}, u32[]{:S(2)}) copy-start(bf16[2048]{0:T(1024)(128)(2,1)} %param.22) | copy-start | bytes 12292
  12.8 22.4 %all-to-all-start = ((bf16[4,16,512]{2,0,1:T(4,128)(2,1)}), bf16[4,16,512]{2,0,1:T(4,128)(2,1)S(1)}, u32[]{:S(2)}, u32[]{:S(2)}) async-start(bf16[4,16,512]{2,0,1:T(4,128)(2,1)} %copy.29), calls=%async_computation | async-start | bytes 131072 | tf_op jit(solution)/shard_map/all_to_all | solution.py:63
  20.2 136.8 %all-reduce.5.cloned.1.call-start = ((), (), s32[]{:S(2)}) async-start(), calls=%async_computation.3 | async-start | bytes 1048576
  34.5 33.3 %copy-start.3 = (bf16[32,2048]{1,0:T(8,128)(2,1)S(1)}, bf16[32,2048]{1,0:T(8,128)(2,1)}, u32[]{:S(2)}) copy-start(bf16[32,2048]{1,0:T(8,128)(2,1)} %param.21) | copy-start | bytes 393220
  65.7 91.3 %copy-start.2 = (bf16[4,2048]{1,0:T(4,128)(2,1)S(1)}, bf16[4,2048]{1,0:T(4,128)(2,1)}, u32[]{:S(2)}) copy-start(bf16[4,2048]{1,0:T(4,128)(2,1)} %param.17) | copy-start | bytes 49156
  183.2 2.2 copy-start.8
  185.9 6.0 %copy-start.6 = (f32[8,6]{1,0:T(8,128)S(1)}, f32[8,6]{1,0:T(8,128)}, u32[]{:S(2)}) copy-start(f32[8,6]{1,0:T(8,128)} %param.24) | copy-start | bytes 580
  185.9 6.1 %copy-start.10 = (u32[32]{0:T(128)S(1)}, u32[32]{0:T(128)}, u32[]{:S(2)}) copy-start(u32[32]{0:T(128)} %constant.59) | copy-start | bytes 388
  187.8 18.4 %all-to-all-start.2 = ((bf16[16,6,2048]{2,1,0:T(8,128)(2,1)}), bf16[16,6,2048]{2,1,0:T(8,128)(2,1)S(1)}, u32[]{:S(2)}, u32[]{:S(2)}) async-start(bf16[16,6,2048]{2,1,0:T(8,128)(2,1)} %copy.37), calls=%async_computation.2 | async-start | bytes 1048576 | tf_op jit(solution)/shard_map/all_to_all | solution.py:124
Sparse Core Ops, SparseCore 0:
  69.0 87.9 all-reduce.4
where the time goes:
time: 224 us; the launch traced here: 223 us
  waiting for transfers between devices  99.8 us (45%)
  blocking collectives  74.4 us (33%)
  between operations  15.6 us (7%)
  matrix products  12.3 us (5%)
  starting transfers between devices  11.6 us (5%)
  other arithmetic  5.19 us (2%)
  local copies, waits for them, and re-layouts  4.47 us (2%)
    unnamed x2, waiting for transfers between devices  87 us
    psum x1, blocking collectives, local(): adapter_down_rows = lax.psum(adapter_output, 'expert')  30 us
    unnamed x2, blocking collectives  20.7 us
    all_to_all x1, blocking collectives, local(): lax.all_to_all(outgoing, 'expert', split_axis=0, concat_axis=0, tiled=True)  19.2 us
    all_to_all x1, waiting for transfers between devices, local(): lax.all_to_all(partial_value.astype(jnp.bfloat16), 'expert', split_axis=0...  12.8 us
    all_to_all x1, starting transfers between devices, local(): lax.all_to_all(latent_out, 'expert', split_axis=1, concat_axis=0, tiled=T...  7.41 us
  transfers between devices with their start and end apart: 3, of which 2 were waited for; matrix products, arithmetic and copies ran while one was open for 1% of the time, Pallas kernels for 0%

commit v1 on v0

v1 whole, which is shorter than its diff:
```python
import functools

import jax
import jax.numpy as jnp
from jax import lax
from jax.experimental import pallas as pl
from jax.experimental.pallas import tpu as pltpu
from jax.sharding import PartitionSpec as P

LAT = 512
ADAPTER_RANK = 16
SOFTMAX_SCALE = 192.0 ** (-0.5)
ADAPTER_SCALE = 2.0
EPSILON = 1e-06
LANES = 128
MESH = pl.DeviceIdType.MESH
F32 = jnp.float32
BF16 = jnp.bfloat16
NT = (((1,), (1,)), ((), ()))
TN = (((0,), (0,)), ((), ()))


def layer_kernel(
    dims,
    lengths,
    adapter_ids,
    q_hbm,
    cache_hbm,
    residual_hbm,
    value_hbm,
    down_hbm,
    upf_hbm,
    gain_hbm,
    ids_hbm,
    gates_hbm,
    wg_hbm,
    wu_hbm,
    wd_hbm,
    out_ref,
    q,
    cache,
    residual,
    value_out,
    adapter_down,
    up_factors,
    gain,
    ids,
    gates,
    w_gate,
    w_up,
    w_down,
    meta,
    att,
    pieces,
    lora,
    rs1_out,
    rs1_in,
    tok,
    r1_out,
    r1_in,
    r2_out,
    r2_in,
    r3_out,
    r3_in,
    cache_sem,
    load_sem,
    send_sem,
    recv_sem,
    tok_sem,
):
    n_expert, n_dp, top = dims
    n_group = n_expert // 2
    me = lax.axis_index("expert")
    my_dp = lax.axis_index("dp")
    my_group = me // 2
    my_core = lax.rem(me, 2)
    other_core = 1 - my_core
    partner = my_group * 2 + other_core
    rows, model_width = residual.shape
    column = ids.shape[0]
    heads = q.shape[1]
    width = att.shape[2]
    group_rows = n_expert * rows
    lane_rows = lora.shape[2]

    cache_loads = []
    for r in range(rows):
        cache_loads.append(pltpu.make_async_copy(cache_hbm.at[r], cache.at[r], cache_sem.at[r]))
    small = []
    for k, (src, dst) in enumerate(
        (
            (q_hbm, q),
            (ids_hbm, ids),
            (gates_hbm, gates),
            (residual_hbm, residual),
            (gain_hbm, gain),
            (down_hbm, adapter_down),
            (value_hbm, value_out),
            (upf_hbm, up_factors),
            (wg_hbm, w_gate),
            (wu_hbm, w_up),
            (wd_hbm, w_down),
        )
    ):
        small.append(pltpu.make_async_copy(src, dst, load_sem.at[k]))
    small[0].start()
    for load in cache_loads:
        load.start()
    for load in small[1:]:
        load.start()

    barrier = pltpu.get_barrier_semaphore()
    for i in range(1, n_expert):
        pl.semaphore_signal(
            barrier, inc=1, device_id={"expert": lax.rem(me + i, n_expert)}, device_id_type=MESH
        )
    for i in range(1, n_dp):
        pl.semaphore_signal(
            barrier, inc=1, device_id={"dp": lax.rem(my_dp + i, n_dp)}, device_id_type=MESH
        )

    def send(src, dst, sends, recvs, where):
        pltpu.make_async_remote_copy(
            src_ref=src, dst_ref=dst, send_sem=sends, recv_sem=recvs, device_id=where,
            device_id_type=MESH,
        ).start()

    def wait_bytes(ref, sem):
        pltpu.make_async_copy(ref, ref, sem).wait()

    small[0].wait()
    outs = []
    for r in range(rows):
        cache_loads[r].wait()
        keys = cache[r]
        scores = lax.dot_general(q[r], keys, NT, preferred_element_type=F32) * SOFTMAX_SCALE
        position = lax.broadcasted_iota(jnp.int32, scores.shape, 1)
        scores = jnp.where(position < lengths[r], scores, -1e30)
        raised = jnp.exp(scores - jnp.max(scores, axis=1, keepdims=True))
        weights = (raised / jnp.sum(raised, axis=1, keepdims=True)).astype(BF16)
        outs.append(jnp.dot(weights, keys[:, :LAT], preferred_element_type=F32))
    by_head = jnp.stack(outs, axis=1).astype(BF16)
    parts = LAT // width
    if parts == 1:
        att[...] = by_head
    else:
        for h in range(heads):
            for part in range(parts):
                att[h * parts + part] = by_head[h, :, part * width : (part + 1) * width]

    small[1].wait()
    small[2].wait()
    lane = lax.broadcasted_iota(jnp.int32, (column, LANES), 1)
    dense = jnp.zeros((column, LANES), F32)
    for k in range(top):
        dense += jnp.where(lane == ids[:, k : k + 1], gates[:, k : k + 1], 0.0)
    meta[me, 0:column, :] = dense
    row_of = lax.broadcasted_iota(jnp.int32, (8, LANES), 0)
    named = jnp.zeros((8, LANES), jnp.int32)
    for r in range(rows):
        named = jnp.where(row_of == r, adapter_ids[r], named)
    meta[me, column : column + 8, :] = named.astype(F32)

    pl.semaphore_wait(barrier, n_expert - 1 + n_dp - 1)
    for i in range(1, n_expert):
        to = lax.rem(me + i, n_expert)
        send(att.at[to], pieces.at[me], send_sem.at[0], recv_sem.at[0], {"expert": to})
        mine = meta.at[me]
        send(mine, mine, send_sem.at[1], recv_sem.at[1], {"expert": to})
    pieces[me] = att[me]

    small[5].wait()
    wait_bytes(pieces.at[0 : n_expert - 1], recv_sem.at[0])
    latent = pieces[...].reshape(group_rows, width)
    wait_bytes(meta.at[0 : n_expert - 1], recv_sem.at[1])
    adapter_of = (
        meta[:, column : column + rows, :].reshape(group_rows, LANES)
    )
    full = jnp.dot(latent, adapter_down[...], preferred_element_type=F32)
    of_column = lax.broadcasted_iota(jnp.int32, full.shape, 1) // ADAPTER_RANK
    chosen = jnp.where(of_column.astype(F32) == adapter_of[:, 0:1], full, 0.0)
    high = chosen.astype(BF16)
    low = (chosen - high.astype(F32)).astype(BF16)
    fold_shape = (ADAPTER_RANK, full.shape[1])
    fold = (
        lax.rem(lax.broadcasted_iota(jnp.int32, fold_shape, 1), ADAPTER_RANK)
        == lax.broadcasted_iota(jnp.int32, fold_shape, 0)
    ).astype(F32).astype(BF16)
    down_part = lax.dot_general(fold, high, NT, preferred_element_type=F32) + lax.dot_general(
        fold, low, NT, preferred_element_type=F32
    )
    if lane_rows > group_rows:
        down_part = jnp.concatenate(
            [down_part, jnp.zeros((ADAPTER_RANK, lane_rows - group_rows), F32)], axis=1
        )
    lora[me] = down_part
    for i in range(1, n_expert):
        to = lax.rem(me + i, n_expert)
        send(lora.at[me], lora.at[me], send_sem.at[2], recv_sem.at[2], {"expert": to})

    small[6].wait()
    base = jnp.dot(latent, value_out[...], preferred_element_type=F32)
    small[7].wait()
    if lane_rows > group_rows:
        adapter_of = jnp.concatenate(
            [adapter_of, jnp.zeros((lane_rows - group_rows, LANES), F32)], axis=0
        )
    adapter_lane = adapter_of.T[0:1, :]
    wait_bytes(lora.at[0 : n_expert - 1], recv_sem.at[2])
    scaled = (ADAPTER_SCALE * jnp.sum(lora[...], axis=0)).astype(BF16).astype(F32)
    owned = up_factors.shape[0] // ADAPTER_RANK
    spread = []
    for o in range(owned):
        holds = adapter_lane == (me * owned + o).astype(F32)
        spread.append(jnp.where(holds, scaled, 0.0))
    spread = jnp.concatenate(spread, axis=0).astype(BF16)[:, :group_rows]
    base += lax.dot_general(spread, up_factors[...], TN, preferred_element_type=F32)
    rs1_out[...] = base.reshape(n_expert, rows, model_width).astype(BF16)
    for i in range(1, n_expert):
        to = lax.rem(me + i, n_expert)
        send(rs1_out.at[to], rs1_in.at[me], send_sem.at[3], recv_sem.at[3], {"expert": to})
    rs1_in[me] = rs1_out[me]
    small[3].wait()
    small[4].wait()
    wait_bytes(rs1_in.at[0 : n_expert - 1], recv_sem.at[3])
    attention = jnp.sum(rs1_in[...].astype(F32), axis=0)
    stream = residual[...].astype(F32) + attention
    inverse_rms = lax.rsqrt(jnp.mean(stream * stream, axis=1, keepdims=True) + EPSILON)
    normed = stream * inverse_rms * gain[...].astype(F32)
    tok[my_core, my_dp, my_group] = normed.astype(BF16)

    def block(core, dp, group):
        return tok.at[core, dp, group], tok_sem.at[dp * n_group + group]

    own, own_sem = block(my_core, my_dp, my_group)
    for i in range(1, n_group):
        to = lax.rem(my_group + i, n_group) * 2 + my_core
        send(own, own, send_sem.at[4], own_sem, {"expert": to})
    for i in range(n_group):
        group = lax.rem(my_group + n_group - i, n_group)
        here, here_sem = block(my_core, my_dp, group)
        if i > 0:
            wait_bytes(here, here_sem)
        for j in range(1, n_dp):
            send(here, here, send_sem.at[5], here_sem, {"dp": lax.rem(my_dp + j, n_dp)})
        send(here, here, send_sem.at[6], recv_sem.at[4], {"expert": partner})
    for j in range(1, n_dp):
        from_dp = lax.rem(my_dp + n_dp - j, n_dp)
        for i in range(n_group):
            group = lax.rem(my_group + n_group - i, n_group)
            here, here_sem = block(my_core, from_dp, group)
            wait_bytes(here, here_sem)
            send(here, here, send_sem.at[6], recv_sem.at[4], {"expert": partner})

    def produce(core):
        tokens = tok[core].reshape(n_dp * n_group * rows, model_width)
        weight = []
        for dp in range(n_dp):
            of_rows = meta[pl.ds(core, n_group, stride=2), dp * rows : (dp + 1) * rows, :]
            of_rows = of_rows.reshape(n_group * rows, LANES)
            lanes = lax.broadcasted_iota(jnp.int32, of_rows.shape, 1)
            weight.append(jnp.sum(jnp.where(lanes == me, of_rows, 0.0), axis=1, keepdims=True))
        weight = jnp.concatenate(weight, axis=0)
        gate_act = jnp.dot(tokens, w_gate[0], preferred_element_type=F32)
        up_act = jnp.dot(tokens, w_up[0], preferred_element_type=F32)
        hidden = (gate_act / (1.0 + jnp.exp(-gate_act)) * up_act).astype(BF16)
        made = lax.dot_general(hidden, w_down[0], NT, preferred_element_type=F32)
        return (made * weight).reshape(n_dp, n_group, rows, model_width)

    for k in (8, 9, 10):
        small[k].wait()
    wait_bytes(tok.at[0], recv_sem.at[4])
    r1_out[...] = produce(other_core).astype(BF16)
    send(r1_out, r1_in, send_sem.at[7], recv_sem.at[5], {"expert": partner})
    kept = produce(my_core)
    r2_out[...] = kept.astype(BF16)
    wait_bytes(r1_in, recv_sem.at[5])
    r2_out[...] = (r2_out[...].astype(F32) + r1_in[...].astype(F32)).astype(BF16)
    for j in range(1, n_dp):
        to = lax.rem(my_dp + j, n_dp)
        send(r2_out.at[to], r2_in.at[my_dp], send_sem.at[8], recv_sem.at[6], {"dp": to})
    r2_in[my_dp] = r2_out[my_dp]
    if n_dp > 1:
        wait_bytes(r2_in.at[0 : n_dp - 1], recv_sem.at[6])
    r3_out[...] = jnp.sum(r2_in[...].astype(F32), axis=0).astype(BF16)
    for i in range(1, n_group):
        to = lax.rem(my_group + i, n_group)
        send(
            r3_out.at[to], r3_in.at[my_group], send_sem.at[9], recv_sem.at[7],
            {"expert": to * 2 + my_core},
        )
    r3_in[my_group] = r3_out[my_group]
    wait_bytes(r3_in.at[0 : n_group - 1], recv_sem.at[7])
    routed = jnp.sum(r3_in[...].astype(F32), axis=0)
    out_ref[...] = (stream + routed).astype(BF16)

    wait_bytes(att.at[0 : n_expert - 1], send_sem.at[0])
    wait_bytes(meta.at[0 : n_expert - 1], send_sem.at[1])
    wait_bytes(lora.at[0 : n_expert - 1], send_sem.at[2])
    wait_bytes(rs1_out.at[0 : n_expert - 1], send_sem.at[3])
    wait_bytes(tok.at[0, 0, 0 : n_group - 1], send_sem.at[4])
    if n_dp > 1:
        wait_bytes(tok.at[0, 0 : n_dp - 1], send_sem.at[5])
        wait_bytes(r2_out.at[0 : n_dp - 1], send_sem.at[8])
    wait_bytes(tok.at[0], send_sem.at[6])
    wait_bytes(r1_out, send_sem.at[7])
    wait_bytes(r3_out.at[0 : n_group - 1], send_sem.at[9])


def local(
    n_expert,
    n_dp,
    q_latent,
    latent_cache,
    lengths,
    residual,
    adapter_ids,
    value_out,
    adapter_down,
    adapter_up_factors,
    norm_gain,
    expert_ids,
    gate_weights,
    w_gate,
    w_up,
    w_down,
):
    rows, model_width = residual.shape
    column, top = expert_ids.shape
    heads = q_latent.shape[1]
    width = heads * LAT // n_expert
    n_group = n_expert // 2
    lane_rows = -(-n_expert * rows // LANES) * LANES
    gain = norm_gain.reshape(1, model_width)
    big = (
        q_latent,
        latent_cache,
        residual,
        value_out,
        adapter_down,
        adapter_up_factors,
        gain,
        expert_ids,
        gate_weights,
        w_gate,
        w_up,
        w_down,
    )
    any_spec = pl.BlockSpec(memory_space=pl.ANY)
    smem_spec = pl.BlockSpec(memory_space=pltpu.SMEM)
    dma = pltpu.SemaphoreType.DMA
    all_rows = (n_dp, n_group, rows, model_width)
    return pl.pallas_call(
        functools.partial(layer_kernel, (n_expert, n_dp, top)),
        out_shape=jax.ShapeDtypeStruct((rows, model_width), BF16),
        in_specs=[smem_spec] * 2 + [any_spec] * len(big),
        out_specs=pl.BlockSpec(memory_space=pltpu.VMEM),
        scratch_shapes=[pltpu.VMEM(a.shape, a.dtype) for a in big]
        + [
            pltpu.VMEM((n_expert, column + 8, LANES), F32),
            pltpu.VMEM((n_expert, rows, width), BF16),
            pltpu.VMEM((n_expert, rows, width), BF16),
            pltpu.VMEM((n_expert, ADAPTER_RANK, lane_rows), F32),
            pltpu.VMEM((n_expert, rows, model_width), BF16),
            pltpu.VMEM((n_expert, rows, model_width), BF16),
            pltpu.VMEM((2,) + all_rows, BF16),
            pltpu.VMEM(all_rows, BF16),
            pltpu.VMEM(all_rows, BF16),
            pltpu.VMEM(all_rows, BF16),
            pltpu.VMEM(all_rows, BF16),
            pltpu.VMEM(all_rows[1:], BF16),
            pltpu.VMEM(all_rows[1:], BF16),
            dma((rows,)),
            dma((11,)),
            dma((10,)),
            dma((8,)),
            dma((n_dp * n_group,)),
        ],
        compiler_params=pltpu.CompilerParams(
            collective_id=0, has_side_effects=True, vmem_limit_bytes=64000000
        ),
        name="layer",
    )(lengths, adapter_ids, *big)


def solution(mesh):
    in_specs = (
        P(("expert", "dp"), None, None),
        P(("expert", "dp"), None, None),
        P(("expert", "dp")),
        P(("expert", "dp"), None),
        P(("expert", "dp")),
        P("expert", None),
        P("expert", None),
        P("expert", None),
        P(),
        P("expert", None),
        P("expert", None),
        P("expert", None, "dp"),
        P("expert", None, "dp"),
        P("expert", None, "dp"),
    )
    return jax.shard_map(
        functools.partial(local, mesh.shape["expert"], mesh.shape["dp"]),
        mesh=mesh,
        in_specs=in_specs,
        out_specs=P(("expert", "dp"), None),
        check_vma=False,
    )
```

time: 224 us -> 58.2 us (0.26)
  waiting for transfers between devices: 99.8 us -> 0 us
  blocking collectives: 74.4 us -> 0 us
  Pallas kernels: 0 us -> 51 us
  between operations: 15.6 us -> 0.01 us
  matrix products: 12.3 us -> 0 us
  starting transfers between devices: 11.6 us -> 0 us
  other arithmetic: 5.19 us -> 0 us
  local copies, waits for them, and re-layouts: 4.47 us -> 6.95 us
    unnamed x2 -> x0, waiting for transfers between devices: 87 us -> none
    pallas_call x0 -> x1, Pallas kernels: none -> 51 us  [local(): pl.pallas_call(functools.partial(layer_kernel, (n_expert, n_dp, top)), ou...]
    psum x1 -> x0, blocking collectives: 30 us -> none  [local(): adapter_down_rows = lax.psum(adapter_output, 'expert')]
    unnamed x2 -> x0, blocking collectives: 20.7 us -> none
    all_to_all x1 -> x0, blocking collectives: 19.2 us -> none  [local(): lax.all_to_all(outgoing, 'expert', split_axis=0, concat_axis=0, tiled=True)]
    all_to_all x2 -> x0, waiting for transfers between devices: 12.8 us -> none  [the longest x1 12.8 us: local(): lax.all_to_all(partial_value.astype(jnp.bfloat16), 'expert', split_axis=0...]
    dot_general x10 -> x0, matrix products: 12.3 us -> none  [the longest x1 2.26 us: attend_one(): jnp.dot(weights_bf, latent_rows[:, :LAT], preferred_element_type=jnp.floa...]
    all_to_all x2 -> x0, starting transfers between devices: 11.6 us -> none  [the longest x1 7.41 us: local(): lax.all_to_all(latent_out, 'expert', split_axis=1, concat_axis=0, tiled=T...]
  transfers between devices with their start and end apart: 3 -> 0, of which waited for: 2 -> 0; matrix products, arithmetic and copies ran while one was open for 1% -> 0% of each run, Pallas kernels for 0% -> 0%
where the time goes in v1:
time: 58.2 us; the launch traced here: 57.9 us
  Pallas kernels  51 us (88%)
  local copies, waits for them, and re-layouts  6.95 us (12%)
    pallas_call x1, Pallas kernels, local(): pl.pallas_call(functools.partial(layer_kernel, (n_expert, n_dp, top)), ou...  51 us
    unnamed x2, local copies, waits for them, and re-layouts  5.66 us
    reshape x1, local copies, waits for them, and re-layouts, local(): gain = norm_gain.reshape(1, model_width)  1.29 us

profile of v1, /device:TPU:0, one launch (start us, length us, event | category | flops | bytes accessed | tf_op | source)
XLA Modules:
  0.0 57.9 jit_solution(9170825477702143009)
XLA Ops:
  0.0 1.3 %reshape.3.gain_hbm = bf16[1,2048]{1,0:T(2,128)(2,1)} reshape(bf16[2048]{0:T(1024)(128)(2,1)} %param.22) | data formatting | bytes 8192 | tf_op jit(solution)/shard_map/reshape | solution.py:334
  1.3 4.3 %copy.15.cache_hbm = bf16[4,512,576]{2,1,0:T(8,128)(2,1)} copy(bf16[4,512,576]{1,2,0:T(8,128)(2,1)} %param.15) | data formatting | bytes 4718592 | tf_op args[1]
  5.6 51.0 %layer.1 = bf16[4,2048]{1,0:T(4,128)(2,1)} custom-call(s32[4]{0:T(128)} %lengths.1, s32[4]{0:T(128)} %adapter_ids.1, bf16[4,16,576]{2,1,0:T(8,128)(2,1)} %q_hbm.1, bf16[4,512,576]{2,1,0:T(8,128)(2,1)} %copy.15.cache_hbm, bf16[4,2048]{1,0:T(4,128)(2,1)} %residual_hbm.1, bf16[512,2048]{1,0:T(8,128)(2,1)} %value_hbm.1, bf16[512,512]{1,0:T(8,128)(2,1)} %down_hbm.1, ...), custom_call_target="tpu_custom_call" | custom-call | tf_op jit(solution)/shard_map/layer/pallas_call | solution.py:353
  56.6 1.3 %copy.17 = bf16[4,2048]{1,0:T(4,128)(2,1)} copy(bf16[4,2048]{1,0:T(4,128)(2,1)} %layer.1) | data formatting | bytes 32768

commit v2 on v1

v2 whole, which is shorter than its diff:
```python
import functools

import jax
import jax.numpy as jnp
from jax import lax
from jax.experimental import pallas as pl
from jax.experimental.pallas import tpu as pltpu
from jax.sharding import PartitionSpec as P

LAT = 512
ADAPTER_RANK = 16
SOFTMAX_SCALE = 192.0 ** (-0.5)
ADAPTER_SCALE = 2.0
EPSILON = 1e-06
LANES = 128
CHUNKS = 4
MESH = pl.DeviceIdType.MESH
F32 = jnp.float32
BF16 = jnp.bfloat16
NT = (((1,), (1,)), ((), ()))
TN = (((0,), (0,)), ((), ()))


def layer_kernel(
    dims,
    lengths,
    adapter_ids,
    q_hbm,
    cache_hbm,
    residual_hbm,
    value_hbm,
    down_hbm,
    upf_hbm,
    gain_hbm,
    ids_hbm,
    gates_hbm,
    wg_hbm,
    wu_hbm,
    wd_hbm,
    out_ref,
    q,
    cache,
    residual,
    value_out,
    adapter_down,
    up_factors,
    gain,
    ids,
    gates,
    w_gate,
    w_up,
    w_down,
    names,
    dense_gates,
    att,
    pieces,
    lora,
    a1_out,
    a1_in,
    a2_out,
    a2_in,
    tok,
    r1_out,
    r1_in,
    r2_out,
    r2_in,
    r3_out,
    r3_in,
    cache_sem,
    load_sem,
    send_sem,
    recv_sem,
    tok_sem,
    chunk_send,
    chunk_recv,
):
    n_expert, n_dp, top = dims
    n_group = n_expert // 2
    me = lax.axis_index("expert")
    my_dp = lax.axis_index("dp")
    my_group = me // 2
    my_core = lax.rem(me, 2)
    other_core = 1 - my_core
    partner = my_group * 2 + other_core
    rows, model_width = residual.shape
    column = ids.shape[0]
    heads = q.shape[1]
    width = att.shape[2]
    group_rows = n_expert * rows
    chunks = a1_out.shape[0]
    chunk = model_width // chunks
    packed = ADAPTER_RANK // lora.shape[1]

    cache_loads = []
    for r in range(rows):
        cache_loads.append(pltpu.make_async_copy(cache_hbm.at[r], cache.at[r], cache_sem.at[r]))
    small = []
    for k, (src, dst) in enumerate(
        (
            (q_hbm, q),
            (ids_hbm, ids),
            (gates_hbm, gates),
            (residual_hbm, residual),
            (gain_hbm, gain),
            (down_hbm, adapter_down),
            (value_hbm, value_out),
            (upf_hbm, up_factors),
            (wg_hbm, w_gate),
            (wu_hbm, w_up),
            (wd_hbm, w_down),
        )
    ):
        small.append(pltpu.make_async_copy(src, dst, load_sem.at[k]))
    small[0].start()
    for load in cache_loads:
        load.start()
    for load in small[1:]:
        load.start()

    barrier = pltpu.get_barrier_semaphore()
    for i in range(1, n_expert):
        pl.semaphore_signal(
            barrier, inc=1, device_id={"expert": lax.rem(me + i, n_expert)}, device_id_type=MESH
        )
    for i in range(1, n_dp):
        pl.semaphore_signal(
            barrier, inc=1, device_id={"dp": lax.rem(my_dp + i, n_dp)}, device_id_type=MESH
        )

    def send(src, dst, sends, recvs, where):
        pltpu.make_async_remote_copy(
            src_ref=src, dst_ref=dst, send_sem=sends, recv_sem=recvs, device_id=where,
            device_id_type=MESH,
        ).start()

    def wait_bytes(ref, sem):
        pltpu.make_async_copy(ref, ref, sem).wait()

    small[0].wait()
    outs = []
    for r in range(rows):
        cache_loads[r].wait()
        keys = cache[r]
        scores = jnp.dot(q[r], keys, preferred_element_type=F32) * SOFTMAX_SCALE
        position = lax.broadcasted_iota(jnp.int32, scores.shape, 1)
        scores = jnp.where(position < lengths[r], scores, -1e30)
        raised = jnp.exp(scores - jnp.max(scores, axis=1, keepdims=True))
        weights = (raised / jnp.sum(raised, axis=1, keepdims=True)).astype(BF16)
        outs.append(lax.dot_general(weights, keys[:LAT], NT, preferred_element_type=F32))
    by_head = jnp.stack(outs, axis=1).astype(BF16)
    parts = LAT // width
    if parts == 1:
        att[...] = by_head
    else:
        for h in range(heads):
            for part in range(parts):
                att[h * parts + part] = by_head[h, :, part * width : (part + 1) * width]

    pl.semaphore_wait(barrier, n_expert - 1 + n_dp - 1)
    peers = [lax.rem(me + i, n_expert) for i in range(1, n_expert)]
    for to in peers:
        send(att.at[to], pieces.at[me], send_sem.at[0], recv_sem.at[0], {"expert": to})
    row_of = lax.broadcasted_iota(jnp.int32, (rows, LANES), 0)
    named = jnp.zeros((rows, LANES), jnp.int32)
    for r in range(rows):
        named = jnp.where(row_of == r, adapter_ids[r], named)
    names[me] = named.astype(F32)
    for to in peers:
        send(names.at[me], names.at[me], send_sem.at[1], recv_sem.at[1], {"expert": to})
    pieces[me] = att[me]

    small[5].wait()
    fold_shape = (ADAPTER_RANK, adapter_down.shape[1])
    fold = (
        lax.rem(lax.broadcasted_iota(jnp.int32, fold_shape, 1), ADAPTER_RANK)
        == lax.broadcasted_iota(jnp.int32, fold_shape, 0)
    ).astype(F32).astype(BF16)
    wait_bytes(pieces.at[0 : n_expert - 1], recv_sem.at[0])
    latent = pieces[...].reshape(group_rows, width)
    full = jnp.dot(latent, adapter_down[...], preferred_element_type=F32)
    of_column = lax.broadcasted_iota(jnp.int32, full.shape, 1) // ADAPTER_RANK
    wait_bytes(names.at[0 : n_expert - 1], recv_sem.at[1])
    adapter_of = names[...].reshape(group_rows, LANES)
    chosen = jnp.where(of_column.astype(F32) == adapter_of[:, 0:1], full, 0.0)
    high = chosen.astype(BF16)
    low = (chosen - high.astype(F32)).astype(BF16)
    down_part = lax.dot_general(fold, high, NT, preferred_element_type=F32) + lax.dot_general(
        fold, low, NT, preferred_element_type=F32
    )
    if packed == 2:
        half = ADAPTER_RANK // 2
        down_part = jnp.concatenate([down_part[:half], down_part[half:]], axis=1)
    lora[me] = down_part
    for to in peers:
        send(lora.at[me], lora.at[me], send_sem.at[2], recv_sem.at[2], {"expert": to})

    small[1].wait()
    small[2].wait()
    lane = lax.broadcasted_iota(jnp.int32, (column, LANES), 1)
    dense = jnp.zeros((column, LANES), F32)
    for k in range(top):
        dense += jnp.where(lane == ids[:, k : k + 1], gates[:, k : k + 1], 0.0)
    dense_gates[me] = dense
    for to in peers:
        mine = dense_gates.at[me]
        send(mine, mine, send_sem.at[3], recv_sem.at[3], {"expert": to})

    small[6].wait()
    base = jnp.dot(latent, value_out[...], preferred_element_type=F32)
    small[7].wait()
    small[3].wait()
    small[4].wait()
    pad_rows = -group_rows % LANES
    if pad_rows:
        adapter_of = jnp.concatenate([adapter_of, jnp.zeros((pad_rows, LANES), F32)], axis=0)
    adapter_lane = adapter_of.T[0:1, :group_rows]
    wait_bytes(lora.at[0 : n_expert - 1], recv_sem.at[2])
    scaled = (ADAPTER_SCALE * jnp.sum(lora[...], axis=0)).astype(BF16).astype(F32)
    if packed == 2:
        scaled = jnp.concatenate([scaled[:, :group_rows], scaled[:, group_rows:]], axis=0)
    owned = up_factors.shape[0] // ADAPTER_RANK
    spread = []
    for o in range(owned):
        holds = adapter_lane == (me * owned + o).astype(F32)
        spread.append(jnp.where(holds, scaled, 0.0))
    spread = jnp.concatenate(spread, axis=0).astype(BF16)

    groups = [lax.rem(my_group + i, n_group) for i in range(1, n_group)]
    for k in range(chunks):
        columns = slice(k * chunk, (k + 1) * chunk)
        projected = base[:, columns] + lax.dot_general(
            spread, up_factors[:, columns], TN, preferred_element_type=F32
        )
        projected = projected.reshape(n_group, 2, rows, chunk).astype(BF16)
        for core in range(2):
            a1_out[k, core] = projected[:, core]
        send(
            a1_out.at[k, other_core], a1_in.at[k], chunk_send.at[0, k], chunk_recv.at[0, k],
            {"expert": partner},
        )
    for k in range(chunks):
        wait_bytes(a1_in.at[k], chunk_recv.at[0, k])
        a2_out[k] = (a1_out[k, my_core].astype(F32) + a1_in[k].astype(F32)).astype(BF16)
        for to in groups:
            send(
                a2_out.at[k, to], a2_in.at[k, my_group], chunk_send.at[1, k], chunk_recv.at[1, k],
                {"expert": to * 2 + my_core},
            )
        a2_in[k, my_group] = a2_out[k, my_group]
    attention = []
    for k in range(chunks):
        wait_bytes(a2_in.at[k, 0 : n_group - 1], chunk_recv.at[1, k])
        attention.append(jnp.sum(a2_in[k].astype(F32), axis=0))
    stream = residual[...].astype(F32) + jnp.concatenate(attention, axis=1)
    inverse_rms = lax.rsqrt(jnp.mean(stream * stream, axis=1, keepdims=True) + EPSILON)
    normed = stream * inverse_rms * gain[...].reshape(1, model_width).astype(F32)
    tok[my_core, my_dp, my_group] = normed.astype(BF16)

    def block(core, dp, group):
        return tok.at[core, dp, group], tok_sem.at[dp * n_group + group]

    own, own_sem = block(my_core, my_dp, my_group)
    for i in range(1, n_group):
        to = lax.rem(my_group + i, n_group) * 2 + my_core
        send(own, own, send_sem.at[4], own_sem, {"expert": to})
    for i in range(n_group):
        group = lax.rem(my_group + n_group - i, n_group)
        here, here_sem = block(my_core, my_dp, group)
        if i > 0:
            wait_bytes(here, here_sem)
        for j in range(1, n_dp):
            send(here, here, send_sem.at[5], here_sem, {"dp": lax.rem(my_dp + j, n_dp)})
        send(here, here, send_sem.at[6], recv_sem.at[4], {"expert": partner})
    for j in range(1, n_dp):
        from_dp = lax.rem(my_dp + n_dp - j, n_dp)
        for i in range(n_group):
            group = lax.rem(my_group + n_group - i, n_group)
            here, here_sem = block(my_core, from_dp, group)
            wait_bytes(here, here_sem)
            send(here, here, send_sem.at[6], recv_sem.at[4], {"expert": partner})

    all_rows = 2 * n_dp * n_group * rows
    wait_bytes(dense_gates.at[0 : n_expert - 1], recv_sem.at[3])
    weight = []
    for core in range(2):
        for dp in range(n_dp):
            of_rows = dense_gates[
                pl.ds(core, n_group, stride=2), dp * rows : (dp + 1) * rows, :
            ].reshape(n_group * rows, LANES)
            lanes = lax.broadcasted_iota(jnp.int32, of_rows.shape, 1)
            weight.append(jnp.sum(jnp.where(lanes == me, of_rows, 0.0), axis=1, keepdims=True))
    weight = jnp.concatenate(weight, axis=0)
    for k in (8, 9, 10):
        small[k].wait()
    wait_bytes(tok.at[0], recv_sem.at[4])
    tokens = tok[...].reshape(all_rows, model_width)
    gate_act = jnp.dot(tokens, w_gate[0], preferred_element_type=F32)
    up_act = jnp.dot(tokens, w_up[0], preferred_element_type=F32)
    hidden = (gate_act / (1.0 + jnp.exp(-gate_act)) * up_act).astype(BF16)

    for k in range(chunks):
        made = lax.dot_general(
            hidden, w_down[0, k * chunk : (k + 1) * chunk, :], NT, preferred_element_type=F32
        )
        r1_out[k] = (made * weight).reshape(2, n_dp, n_group, rows, chunk).astype(BF16)
        send(
            r1_out.at[k, other_core], r1_in.at[k], chunk_send.at[2, k], chunk_recv.at[2, k],
            {"expert": partner},
        )
    for k in range(chunks):
        wait_bytes(r1_in.at[k], chunk_recv.at[2, k])
        r2_out[k] = (r1_out[k, my_core].astype(F32) + r1_in[k].astype(F32)).astype(BF16)
        for j in range(1, n_dp):
            to = lax.rem(my_dp + j, n_dp)
            send(
                r2_out.at[k, to], r2_in.at[k, my_dp], chunk_send.at[3, k], chunk_recv.at[3, k],
                {"dp": to},
            )
        r2_in[k, my_dp] = r2_out[k, my_dp]
    for k in range(chunks):
        if n_dp > 1:
            wait_bytes(r2_in.at[k, 0 : n_dp - 1], chunk_recv.at[3, k])
        r3_out[k] = jnp.sum(r2_in[k].astype(F32), axis=0).astype(BF16)
        for to in groups:
            send(
                r3_out.at[k, to], r3_in.at[k, my_group], chunk_send.at[4, k], chunk_recv.at[4, k],
                {"expert": to * 2 + my_core},
            )
        r3_in[k, my_group] = r3_out[k, my_group]
    for k in range(chunks):
        wait_bytes(r3_in.at[k, 0 : n_group - 1], chunk_recv.at[4, k])
        routed = jnp.sum(r3_in[k].astype(F32), axis=0)
        columns = slice(k * chunk, (k + 1) * chunk)
        out_ref[:, columns] = (stream[:, columns] + routed).astype(BF16)

    for k, ref in enumerate((att, names, lora, dense_gates)):
        wait_bytes(ref.at[0 : n_expert - 1], send_sem.at[k])
    wait_bytes(tok.at[0, 0, 0 : n_group - 1], send_sem.at[4])
    if n_dp > 1:
        wait_bytes(tok.at[0, 0 : n_dp - 1], send_sem.at[5])
    wait_bytes(tok.at[0], send_sem.at[6])
    for k in range(chunks):
        wait_bytes(a1_in.at[k], chunk_send.at[0, k])
        wait_bytes(a2_out.at[k, 0 : n_group - 1], chunk_send.at[1, k])
        wait_bytes(r1_in.at[k], chunk_send.at[2, k])
        if n_dp > 1:
            wait_bytes(r2_out.at[k, 0 : n_dp - 1], chunk_send.at[3, k])
        wait_bytes(r3_out.at[k, 0 : n_group - 1], chunk_send.at[4, k])


def local(
    n_expert,
    n_dp,
    q_latent,
    latent_cache,
    lengths,
    residual,
    adapter_ids,
    value_out,
    adapter_down,
    adapter_up_factors,
    norm_gain,
    expert_ids,
    gate_weights,
    w_gate,
    w_up,
    w_down,
):
    rows, model_width = residual.shape
    column, top = expert_ids.shape
    heads = q_latent.shape[1]
    width = heads * LAT // n_expert
    n_group = n_expert // 2
    packed = 2 if n_expert * rows * 2 == LANES else 1
    lane_rows = packed * n_expert * rows
    chunks = CHUNKS
    chunk = model_width // chunks
    big = (
        q_latent,
        latent_cache.swapaxes(1, 2),
        residual,
        value_out,
        adapter_down,
        adapter_up_factors,
        norm_gain,
        expert_ids,
        gate_weights,
        w_gate,
        w_up,
        w_down,
    )
    any_spec = pl.BlockSpec(memory_space=pl.ANY)
    smem_spec = pl.BlockSpec(memory_space=pltpu.SMEM)
    dma = pltpu.SemaphoreType.DMA
    to_groups = (n_group, rows, chunk)
    to_all = (n_dp,) + to_groups
    return pl.pallas_call(
        functools.partial(layer_kernel, (n_expert, n_dp, top)),
        out_shape=jax.ShapeDtypeStruct((rows, model_width), BF16),
        in_specs=[smem_spec] * 2 + [any_spec] * len(big),
        out_specs=pl.BlockSpec(memory_space=pltpu.VMEM),
        scratch_shapes=[pltpu.VMEM(a.shape, a.dtype) for a in big]
        + [
            pltpu.VMEM((n_expert, rows, LANES), F32),
            pltpu.VMEM((n_expert, column, LANES), F32),
            pltpu.VMEM((n_expert, rows, width), BF16),
            pltpu.VMEM((n_expert, rows, width), BF16),
            pltpu.VMEM((n_expert, ADAPTER_RANK // packed, lane_rows), F32),
            pltpu.VMEM((chunks, 2) + to_groups, BF16),
            pltpu.VMEM((chunks,) + to_groups, BF16),
            pltpu.VMEM((chunks,) + to_groups, BF16),
            pltpu.VMEM((chunks,) + to_groups, BF16),
            pltpu.VMEM((2, n_dp, n_group, rows, model_width), BF16),
            pltpu.VMEM((chunks, 2) + to_all, BF16),
            pltpu.VMEM((chunks,) + to_all, BF16),
            pltpu.VMEM((chunks,) + to_all, BF16),
            pltpu.VMEM((chunks,) + to_all, BF16),
            pltpu.VMEM((chunks,) + to_groups, BF16),
            pltpu.VMEM((chunks,) + to_groups, BF16),
            dma((rows,)),
            dma((11,)),
            dma((10,)),
            dma((8,)),
            dma((n_dp * n_group,)),
            dma((5, chunks)),
            dma((5, chunks)),
        ],
        compiler_params=pltpu.CompilerParams(
            collective_id=0, has_side_effects=True, vmem_limit_bytes=64000000
        ),
        name="layer",
    )(lengths, adapter_ids, *big)


def solution(mesh):
    in_specs = (
        P(("expert", "dp"), None, None),
        P(("expert", "dp"), None, None),
        P(("expert", "dp")),
        P(("expert", "dp"), None),
        P(("expert", "dp")),
        P("expert", None),
        P("expert", None),
        P("expert", None),
        P(),
        P("expert", None),
        P("expert", None),
        P("expert", None, "dp"),
        P("expert", None, "dp"),
        P("expert", None, "dp"),
    )
    return jax.shard_map(
        functools.partial(local, mesh.shape["expert"], mesh.shape["dp"]),
        mesh=mesh,
        in_specs=in_specs,
        out_specs=P(("expert", "dp"), None),
        check_vma=False,
    )
```

time: 58.2 us -> 48.2 us (0.83)
  local copies, waits for them, and re-layouts: 6.95 us -> 1.33 us
  Pallas kernels: 51 us -> 46.5 us
    pallas_call x1, Pallas kernels: 51 us -> 46.5 us  [local(): pl.pallas_call(functools.partial(layer_kernel, (n_expert, n_dp, top)), ou...]
    unnamed x2 -> x1, local copies, waits for them, and re-layouts: 5.66 us -> 1.33 us
    reshape x1 -> x0, local copies, waits for them, and re-layouts: 1.29 us -> none  [local(): gain = norm_gain.reshape(1, model_width)]
where the time goes in v2:
time: 48.2 us; the launch traced here: 47.9 us
  Pallas kernels  46.5 us (96%)
  local copies, waits for them, and re-layouts  1.33 us (3%)
    pallas_call x1, Pallas kernels, local(): pl.pallas_call(functools.partial(layer_kernel, (n_expert, n_dp, top)), ou...  46.5 us
    unnamed x1, local copies, waits for them, and re-layouts  1.33 us

profile of v2, /device:TPU:0, one launch (start us, length us, event | category | flops | bytes accessed | tf_op | source)
XLA Modules:
  0.0 47.9 jit_solution(13771081624899827786)
XLA Ops:
  0.0 46.5 %layer.1 = bf16[4,2048]{1,0:T(4,128)(2,1)} custom-call(s32[4]{0:T(128)} %lengths.1, s32[4]{0:T(128)} %adapter_ids.1, bf16[4,16,576]{2,1,0:T(8,128)(2,1)} %q_hbm.1, bf16[4,576,512]{2,1,0:T(8,128)(2,1)} %bitcast.1, bf16[4,2048]{1,0:T(4,128)(2,1)} %residual_hbm.1, bf16[512,2048]{1,0:T(8,128)(2,1)} %value_hbm.1, bf16[512,512]{1,0:T(8,128)(2,1)} %down_hbm.1, ...), custom_call_target="tpu_custom_call" | custom-call | tf_op jit(solution)/shard_map/layer/pallas_call | solution.py:397
  46.6 1.3 %copy.16 = bf16[4,2048]{1,0:T(4,128)(2,1)} copy(bf16[4,2048]{1,0:T(4,128)(2,1)} %layer.1) | data formatting | bytes 32768

commit v3 on v2

--- a/solution.py
+++ b/solution.py
@@ -114,8 +114,6 @@
     small[0].start()
     for load in cache_loads:
         load.start()
-    for load in small[1:]:
-        load.start()
 
     barrier = pltpu.get_barrier_semaphore()
     for i in range(1, n_expert):
@@ -137,16 +135,34 @@
         pltpu.make_async_copy(ref, ref, sem).wait()
 
     small[0].wait()
+    for load in cache_loads:
+        load.wait()
+    for k in (5, 6, 7, 1, 2, 3, 4, 8, 9, 10):
+        small[k].start()
+    all_scores = []
+    for r in range(rows):
+        scores = jnp.dot(q[r], cache[r], preferred_element_type=F32) * SOFTMAX_SCALE
+        position = lax.broadcasted_iota(jnp.int32, scores.shape, 1)
+        all_scores.append(jnp.where(position < lengths[r], scores, -1e30))
+    all_scores = jnp.concatenate(all_scores, axis=0)
+    raised = jnp.exp(all_scores - jnp.max(all_scores, axis=1, keepdims=True))
+    weights = (raised / jnp.sum(raised, axis=1, keepdims=True)).astype(BF16)
+
+    row_of = lax.broadcasted_iota(jnp.int32, (rows, LANES), 0)
+    named = jnp.zeros((rows, LANES), jnp.int32)
+    for r in range(rows):
+        named = jnp.where(row_of == r, adapter_ids[r], named)
+    names[me] = named.astype(F32)
+    peers = [lax.rem(me + i, n_expert) for i in range(1, n_expert)]
+    pl.semaphore_wait(barrier, n_expert - 1 + n_dp - 1)
+    for to in peers:
+        send(names.at[me], names.at[me], send_sem.at[1], recv_sem.at[1], {"expert": to})
     outs = []
     for r in range(rows):
-        cache_loads[r].wait()
-        keys = cache[r]
-        scores = jnp.dot(q[r], keys, preferred_element_type=F32) * SOFTMAX_SCALE
-        position = lax.broadcasted_iota(jnp.int32, scores.shape, 1)
-        scores = jnp.where(position < lengths[r], scores, -1e30)
-        raised = jnp.exp(scores - jnp.max(scores, axis=1, keepdims=True))
-        weights = (raised / jnp.sum(raised, axis=1, keepdims=True)).astype(BF16)
-        outs.append(lax.dot_general(weights, keys[:LAT], NT, preferred_element_type=F32))
+        of_request = weights[r * heads : (r + 1) * heads]
+        outs.append(
+            lax.dot_general(of_request, cache[r, :LAT], NT, preferred_element_type=F32)
+        )
     by_head = jnp.stack(outs, axis=1).astype(BF16)
     parts = LAT // width
     if parts == 1:
@@ -156,17 +172,8 @@
             for part in range(parts):
                 att[h * parts + part] = by_head[h, :, part * width : (part + 1) * width]
 
-    pl.semaphore_wait(barrier, n_expert - 1 + n_dp - 1)
-    peers = [lax.rem(me + i, n_expert) for i in range(1, n_expert)]
     for to in peers:
         send(att.at[to], pieces.at[me], send_sem.at[0], recv_sem.at[0], {"expert": to})
-    row_of = lax.broadcasted_iota(jnp.int32, (rows, LANES), 0)
-    named = jnp.zeros((rows, LANES), jnp.int32)
-    for r in range(rows):
-        named = jnp.where(row_of == r, adapter_ids[r], named)
-    names[me] = named.astype(F32)
-    for to in peers:
-        send(names.at[me], names.at[me], send_sem.at[1], recv_sem.at[1], {"expert": to})
     pieces[me] = att[me]
 
     small[5].wait()

time: 48.2 us -> 46.5 us (0.965)
  Pallas kernels: 46.5 us -> 44.9 us
    pallas_call x1, Pallas kernels: 46.5 us -> 44.9 us  [local(): pl.pallas_call(functools.partial(layer_kernel, (n_expert, n_dp, top)), ou...]
where the time goes in v3:
time: 46.5 us; the launch traced here: 46.3 us
  Pallas kernels  44.9 us (97%)
  local copies, waits for them, and re-layouts  1.33 us (3%)
    pallas_call x1, Pallas kernels, local(): pl.pallas_call(functools.partial(layer_kernel, (n_expert, n_dp, top)), ou...  44.9 us
    unnamed x1, local copies, waits for them, and re-layouts  1.33 us

profile of v3, /device:TPU:0, one launch (start us, length us, event | category | flops | bytes accessed | tf_op | source)
XLA Modules:
  0.0 46.3 jit_solution(12880888143529753684)
XLA Ops:
  0.0 44.9 %layer.1 = bf16[4,2048]{1,0:T(4,128)(2,1)} custom-call(s32[4]{0:T(128)} %lengths.1, s32[4]{0:T(128)} %adapter_ids.1, bf16[4,16,576]{2,1,0:T(8,128)(2,1)} %q_hbm.1, bf16[4,576,512]{2,1,0:T(8,128)(2,1)} %bitcast.1, bf16[4,2048]{1,0:T(4,128)(2,1)} %residual_hbm.1, bf16[512,2048]{1,0:T(8,128)(2,1)} %value_hbm.1, bf16[512,512]{1,0:T(8,128)(2,1)} %down_hbm.1, ...), custom_call_target="tpu_custom_call" | custom-call | tf_op jit(solution)/shard_map/layer/pallas_call | solution.py:404
  45.0 1.3 %copy.16 = bf16[4,2048]{1,0:T(4,128)(2,1)} copy(bf16[4,2048]{1,0:T(4,128)(2,1)} %layer.1) | data formatting | bytes 32768

commit v4 on v3

--- a/solution.py
+++ b/solution.py
@@ -82,6 +82,7 @@
     my_core = lax.rem(me, 2)
     other_core = 1 - my_core
     partner = my_group * 2 + other_core
+    far_first = sorted(range(1, n_group), key=lambda i: -min(i, n_group - i))
     rows, model_width = residual.shape
     column = ids.shape[0]
     heads = q.shape[1]
@@ -232,7 +233,7 @@
         spread.append(jnp.where(holds, scaled, 0.0))
     spread = jnp.concatenate(spread, axis=0).astype(BF16)
 
-    groups = [lax.rem(my_group + i, n_group) for i in range(1, n_group)]
+    groups = [lax.rem(my_group + i, n_group) for i in far_first]
     for k in range(chunks):
         columns = slice(k * chunk, (k + 1) * chunk)
         projected = base[:, columns] + lax.dot_general(
@@ -267,7 +268,7 @@
         return tok.at[core, dp, group], tok_sem.at[dp * n_group + group]
 
     own, own_sem = block(my_core, my_dp, my_group)
-    for i in range(1, n_group):
+    for i in far_first:
         to = lax.rem(my_group + i, n_group) * 2 + my_core
         send(own, own, send_sem.at[4], own_sem, {"expert": to})
     for i in range(n_group):

time: 46.5 us -> 46.6 us (level)
  no operation moved by 1% of the time
where the time goes in v4:
time: 46.6 us; the launch traced here: 46.3 us
  Pallas kernels  45 us (97%)
  local copies, waits for them, and re-layouts  1.33 us (3%)
    pallas_call x1, Pallas kernels, local(): pl.pallas_call(functools.partial(layer_kernel, (n_expert, n_dp, top)), ou...  45 us
    unnamed x1, local copies, waits for them, and re-layouts  1.33 us

profile of v4, /device:TPU:0, one launch (start us, length us, event | category | flops | bytes accessed | tf_op | source)
XLA Modules:
  0.0 46.3 jit_solution(10157260890157939040)
XLA Ops:
  0.0 45.0 %layer.1 = bf16[4,2048]{1,0:T(4,128)(2,1)} custom-call(s32[4]{0:T(128)} %lengths.1, s32[4]{0:T(128)} %adapter_ids.1, bf16[4,16,576]{2,1,0:T(8,128)(2,1)} %q_hbm.1, bf16[4,576,512]{2,1,0:T(8,128)(2,1)} %bitcast.1, bf16[4,2048]{1,0:T(4,128)(2,1)} %residual_hbm.1, bf16[512,2048]{1,0:T(8,128)(2,1)} %value_hbm.1, bf16[512,512]{1,0:T(8,128)(2,1)} %down_hbm.1, ...), custom_call_target="tpu_custom_call" | custom-call | tf_op jit(solution)/shard_map/layer/pallas_call | solution.py:405
  45.0 1.3 %copy.16 = bf16[4,2048]{1,0:T(4,128)(2,1)} copy(bf16[4,2048]{1,0:T(4,128)(2,1)} %layer.1) | data formatting | bytes 32768
